TPU v7x, 32 devices: a whole 2x2x4 slice. The times are simulated.
32 devices in a mesh: gx: 8 (over z, y), gy: 4 (over x, core).
Axes of the slice: x: 2, y: 2, z: 4, core: 2. Of those that a mesh axis runs over, the one named last changes fastest.
Arguments:
- rhs: float32 [64, 256, 256], P('gx', 'gy'), may hold values from -12 to 12
- coefs: float32 [13, 64, 256, 256], P(None, 'gx', 'gy'), may hold values from 0 to 1.4, as said below
- shifts: float32 [4], replicated, may hold values from 0.4 to 1.1
Outputs:
- basis: float32 [5, 64, 256, 256], P(None, 'gx', 'gy')
- factor: float32 [5, 5], replicated
- solution: float32 [64, 256, 256], P('gx', 'gy')
- residual: float32 [64, 256, 256], P('gx', 'gy')
Inputs may be any that keep to these rules, and one draw needn't show every extreme that they name: `coefs`: entry 0 lies in 0.6 to 1.4, entries 1 to 6 in 0.02 to 0.22, entries 7 to 12 in 0 to 0.16.
All inputs are finite; a program needn't handle non-finite values.
Results may differ from a plain program's by a relative error of at most 0.00095.
Values sent between devices are 32-bit elements; how exact they have to be, the bound alone decides.
A program may use at most 64 MiB of HBM per device.

v0:
```python
import functools

import jax
import jax.numpy as jnp
from jax import lax
from jax.experimental import pallas as pl
from jax.experimental.pallas import tpu as pltpu
from jax.sharding import PartitionSpec as P

growth = 2.0
MESH = pl.DeviceIdType.MESH
PAD = 8
ROWS = 128


def basis_kernel(
    n_gx, n_gy, shifts, rhs, coefs, v_out, w_out, gram,
    field_v, field_w, weight, part, gx_part, gy_part,
    load_sem, store_sem, xs, xr, ys, yr, gxs, gxr, gys, gyr,
):
    steps = shifts.shape[0]
    nx, ny, nz = rhs.shape
    mine = slice(1, nx + 1)
    body = slice(PAD, PAD + ny)
    gx, gy = lax.axis_index("gx"), lax.axis_index("gy")
    x_up, x_down = lax.rem(gx + 1, n_gx), lax.rem(gx + n_gx - 1, n_gx)
    has_low, has_high = gy > 0, gy < n_gy - 1

    loads = [
        pltpu.make_async_copy(rhs, field_v.at[0, mine, body, :], load_sem.at[0]),
        pltpu.make_async_copy(coefs.at[0:7], weight.at[0:7], load_sem.at[1]),
        pltpu.make_async_copy(coefs.at[7:13], weight.at[7:13], load_sem.at[2]),
    ]
    for load in loads:
        load.start()

    barrier = pltpu.get_barrier_semaphore()

    def greet_gx(d, c):
        pl.semaphore_signal(barrier, inc=1, device_id={"gx": lax.rem(gx + d, n_gx)}, device_id_type=MESH)
        return c

    def greet_gy(d, c):
        pl.semaphore_signal(barrier, inc=1, device_id={"gy": lax.rem(gy + d, n_gy)}, device_id_type=MESH)
        return c

    lax.fori_loop(1, n_gx, greet_gx, 0)
    lax.fori_loop(1, n_gy, greet_gy, 0)

    part[...] = jnp.zeros_like(part)

    def clear(fields, rows):
        for k in range(steps):
            for p in range(1, nx + 1):
                fields[k, p, rows, :] = jnp.zeros((PAD, nz), jnp.float32)

    @pl.when(jnp.logical_not(has_low))
    def _():
        clear(field_v, slice(0, PAD))
        clear(field_w, slice(0, PAD))

    @pl.when(jnp.logical_not(has_high))
    def _():
        clear(field_v, slice(PAD + ny, PAD + ny + PAD))
        clear(field_w, slice(PAD + ny, PAD + ny + PAD))

    pl.semaphore_wait(barrier, n_gx + n_gy - 2)

    def x_copy(fields, k, which, side, source=None):
        slot = 2 * steps * which + 2 * k + side
        if source is None:
            source = fields.at[k, 1 if side == 0 else nx, body, :]
        return pltpu.make_async_remote_copy(
            src_ref=source,
            dst_ref=fields.at[k, nx + 1 if side == 0 else 0, body, :],
            send_sem=xs.at[slot],
            recv_sem=xr.at[slot],
            device_id={"gx": x_down if side == 0 else x_up},
            device_id_type=MESH,
        )

    def y_copy(fields, k, which, side, source=None):
        slot = 2 * steps * which + 2 * k + side
        if source is None:
            source = fields.at[k, mine, slice(PAD, 2 * PAD) if side == 0 else slice(ny, PAD + ny), :]
        return pltpu.make_async_remote_copy(
            src_ref=source,
            dst_ref=fields.at[k, mine, slice(PAD + ny, PAD + ny + PAD) if side == 0 else slice(0, PAD), :],
            send_sem=ys.at[slot],
            recv_sem=yr.at[slot],
            device_id={"gy": jnp.maximum(gy - 1, 0) if side == 0 else jnp.minimum(gy + 1, n_gy - 1)},
            device_id_type=MESH,
        )

    def y_start(fields, k, which, sources=(None, None)):
        @pl.when(has_low)
        def _():
            y_copy(fields, k, which, 0, sources[0]).start()

        @pl.when(has_high)
        def _():
            y_copy(fields, k, which, 1, sources[1]).start()

    def y_arrived(fields, k, which):
        @pl.when(has_low)
        def _():
            y_copy(fields, k, which, 1).wait_recv()

        @pl.when(has_high)
        def _():
            y_copy(fields, k, which, 0).wait_recv()

    def near(fields, k, p, r, rows):
        centre = fields[k, p + 1, PAD + r : PAD + r + rows, :]
        lane = lax.broadcasted_iota(jnp.int32, centre.shape, 1)
        return centre, (
            fields[k, p, PAD + r : PAD + r + rows, :],
            fields[k, p + 2, PAD + r : PAD + r + rows, :],
            fields[k, p + 1, PAD + r - 1 : PAD + r - 1 + rows, :],
            fields[k, p + 1, PAD + r + 1 : PAD + r + 1 + rows, :],
            jnp.where(lane == 0, 0.0, pltpu.roll(centre, 1, 1)),
            jnp.where(lane == nz - 1, 0.0, pltpu.roll(centre, nz - 1, 1)),
        )

    chunk = 32 if ny % 32 == 0 else 8

    def plane_m(k, p):
        for r in range(0, ny, chunk):
            centre, sides = near(field_v, k, p, r, chunk)
            total = weight[0, p, r : r + chunk, :] * centre
            for d in range(6):
                total = total + weight[1 + d, p, r : r + chunk, :] * sides[d]
            field_w[k, p + 1, PAD + r : PAD + r + chunk, :] = total

    def plane_a(k, p):
        shift = shifts[k]
        for r in range(0, ny, chunk):
            centre, sides = near(field_w, k, p, r, chunk)
            total = centre
            for d in range(6):
                total = total - weight[7 + d, p, r : r + chunk, :] * sides[d]
            old = field_v[k, p + 1, PAD + r : PAD + r + chunk, :]
            field_v[k + 1, p + 1, PAD + r : PAD + r + chunk, :] = growth * (total - shift * old)

    def apply(plane, fields, k, which, out, out_k, out_which, send):
        y_arrived(fields, k, which)

        def inner(p, c):
            plane(k, p)
            return c

        lax.fori_loop(1, nx - 1, inner, 0)
        x_copy(fields, k, which, 1).wait_recv()
        plane(k, 0)

        @pl.when(send)
        def _():
            x_copy(out, out_k, out_which, 0).start()

        x_copy(fields, k, which, 0).wait_recv()
        plane(k, nx - 1)

        @pl.when(send)
        def _():
            x_copy(out, out_k, out_which, 1).start()
            y_start(out, out_k, out_which)

    def products(i):
        def one(j, c):
            def add(p, total):
                a = field_v[i, p + 1, body, :]
                b = field_v[j, p + 1, body, :]
                return total + jnp.sum((a * b).reshape(ny // 8, 8, nz), axis=0)

            total = lax.fori_loop(0, nx, add, jnp.zeros((8, nz), jnp.float32))
            row = jnp.sum(total, axis=0, keepdims=True)
            flat = row[:, :ROWS]
            for q in range(1, nz // ROWS):
                flat = flat + row[:, q * ROWS : (q + 1) * ROWS]
            part[pl.ds(i * (steps + 1) + j, 1), :] = flat
            return c

        lax.fori_loop(0, i + 1, one, 0)

    x_copy(field_v, 0, 0, 0, rhs.at[0]).start()
    x_copy(field_v, 0, 0, 1, rhs.at[nx - 1]).start()
    y_start(field_v, 0, 0, (rhs.at[:, 0:PAD, :], rhs.at[:, ny - PAD : ny, :]))
    loads[0].wait()
    products(0)
    loads[1].wait()
    loads[2].wait()

    def v_store(k):
        return pltpu.make_async_copy(field_v.at[k + 1, mine, body, :], v_out.at[k], store_sem.at[0, k])

    def w_store(k):
        return pltpu.make_async_copy(field_w.at[k, mine, body, :], w_out.at[k], store_sem.at[1, k])

    def step(k, c):
        apply(plane_m, field_v, k, 0, field_w, k, 1, k >= 0)
        w_store(k).start()
        apply(plane_a, field_w, k, 1, field_v, k + 1, 0, k + 1 < steps)
        v_store(k).start()
        products(k + 1)
        return c

    lax.fori_loop(0, steps, step, 0)

    def gather(axis, me, n, store, send_sem, recv_sem, value):
        store[me] = value

        def copy(d):
            return pltpu.make_async_remote_copy(
                src_ref=store.at[me],
                dst_ref=store.at[me],
                send_sem=send_sem.at[d],
                recv_sem=recv_sem.at[d],
                device_id={axis: lax.rem(me + d, n)},
                device_id_type=MESH,
            )

        def start(d, c):
            copy(d).start()
            return c

        def arrive(d, c):
            copy(d).wait_recv()
            return c

        def sent(d, c):
            copy(d).wait_send()
            return c

        lax.fori_loop(1, n, start, 0)
        lax.fori_loop(1, n, arrive, 0)
        total = lax.fori_loop(0, n, lambda s, t: t + store[s], jnp.zeros_like(value))
        return total, lambda: lax.fori_loop(1, n, sent, 0)

    total, done_x = gather("gx", gx, n_gx, gx_part, gxs, gxr, part[...])
    total, done_y = gather("gy", gy, n_gy, gy_part, gys, gyr, total)
    gram[...] = total
    done_x()
    done_y()

    def finish(k, c):
        for which, fields in ((0, field_v), (1, field_w)):
            for side in range(2):
                x_copy(fields, k, which, side).wait_send()

            @pl.when(has_low)
            def _():
                y_copy(fields, k, which, 0).wait_send()

            @pl.when(has_high)
            def _():
                y_copy(fields, k, which, 1).wait_send()

        v_store(k).wait()
        w_store(k).wait()
        return c

    lax.fori_loop(0, steps, finish, 0)


def small_algebra(gram, shifts, cells):
    steps = shifts.shape[0]
    order = steps + 1
    sums = jnp.sum(gram, axis=1, keepdims=True) / cells
    sums = jnp.broadcast_to(sums, gram.shape)

    def entry(i, j):
        n = max(i, j) * order + min(i, j)
        return sums[n : n + 1, :]

    factor = {}
    for i in range(order):
        value = entry(i, i)
        for k in range(i):
            value = value - factor[k, i] * factor[k, i]
        factor[i, i] = jnp.sqrt(value)
        for j in range(i + 1, order):
            value = entry(i, j)
            for k in range(i):
                value = value - factor[k, i] * factor[k, j]
            factor[i, j] = value / factor[i, i]
    inverse = {}
    for j in range(order):
        inverse[j, j] = 1.0 / factor[j, j]
        for i in range(j - 1, -1, -1):
            value = factor[i, i + 1] * inverse[i + 1, j]
            for k in range(i + 2, j + 1):
                value = value + factor[i, k] * inverse[k, j]
            inverse[i, j] = -value / factor[i, i]
    zero = jnp.zeros_like(factor[0, 0])

    def upper(i, j):
        return factor.get((i, j), zero)

    hess = [[upper(i, k) * shifts[k] + upper(i, k + 1) * (1.0 / growth) for k in range(steps)] for i in range(order)]
    target = [upper(i, 0) for i in range(order)]
    for k in range(steps):
        top, below = hess[k][k], hess[k + 1][k]
        radius = jnp.sqrt(top * top + below * below)
        cosine, sine = top / radius, below / radius
        for c in range(k, steps):
            a, b = hess[k][c], hess[k + 1][c]
            hess[k][c] = cosine * a + sine * b
            hess[k + 1][c] = cosine * b - sine * a
        a, b = target[k], target[k + 1]
        target[k] = cosine * a + sine * b
        target[k + 1] = cosine * b - sine * a
    weights = [None] * steps
    for i in range(steps - 1, -1, -1):
        value = target[i]
        for k in range(i + 1, steps):
            value = value - hess[i][k] * weights[k]
        weights[i] = value / hess[i][i]
    combine = []
    for j in range(order):
        value = zero + (1.0 if j == 0 else 0.0)
        if j < steps:
            value = value - shifts[j] * weights[j]
        if j > 0:
            value = value - (1.0 / growth) * weights[j - 1]
        combine.append(value)
    return factor, inverse, weights, combine


def combine_kernel(cells, shifts, gram, rhs, v, w, basis, factor_out, solution_out, residual, table):
    steps = shifts.shape[0]
    order = steps + 1
    pairs = [(j, k) for k in range(order) for j in range(k + 1)]
    tail = len(pairs)

    @pl.when(pl.program_id(0) == 0)
    def _():
        factor, inverse, weights, combine = small_algebra(gram[...], shifts, cells)
        values = [inverse[p] for p in pairs] + weights + combine
        for n, value in enumerate(values):
            table[n] = jnp.broadcast_to(value, table.shape[1:])
        row = lax.broadcasted_iota(jnp.int32, (8, ROWS), 0)
        column = lax.broadcasted_iota(jnp.int32, (8, ROWS), 1)
        whole = jnp.zeros((8, ROWS), jnp.float32)
        for (i, j), value in factor.items():
            whole = jnp.where((row == i) & (column == j), value, whole)
        factor_out[...] = whole[:order, :order]

    planes, ny, nz = rhs.shape

    def mul(n, x):
        return table[n][None] * x

    def tile(t, c):
        p, r = t // (ny // 16), lax.rem(t, ny // 16) * 16
        rows = pl.ds(pl.multiple_of(r, 16), 16)
        for q in range(0, nz, ROWS):
            lanes = slice(q, q + ROWS)
            at = (p, rows, lanes)
            load = lambda x: x.reshape(2, 8, ROWS)
            fields = [load(rhs[at])] + [load(v[k, p, rows, lanes]) for k in range(steps)]
            for k in range(order):
                total = None
                for j in range(k + 1):
                    term = mul(pairs.index((j, k)), fields[j])
                    total = term if total is None else total + term
                basis[k, p, rows, lanes] = total.reshape(16, ROWS)
            total = mul(tail, load(w[0, p, rows, lanes]))
            for k in range(1, steps):
                total = total + mul(tail + k, load(w[k, p, rows, lanes]))
            solution_out[at] = total.reshape(16, ROWS)
            total = mul(tail + steps, fields[0])
            for j in range(1, order):
                total = total + mul(tail + steps + j, fields[j])
            residual[at] = total.reshape(16, ROWS)
        return c

    lax.fori_loop(0, planes * (ny // 16), tile, 0)


def device_body(n_gx, n_gy, rhs, coefs, shifts):
    steps = shifts.shape[0]
    order = steps + 1
    nx, ny, nz = rhs.shape
    f32 = jnp.float32
    grown = (nx + 2, ny + 2 * PAD, nz)
    table_rows = -(-order * order // 8) * 8
    any_space = pl.BlockSpec(memory_space=pl.ANY)
    smem = pl.BlockSpec(memory_space=pltpu.SMEM)
    vmem = pl.BlockSpec(memory_space=pltpu.VMEM)
    dma = pltpu.SemaphoreType.DMA
    v, w, gram = pl.pallas_call(
        functools.partial(basis_kernel, n_gx, n_gy),
        out_shape=(
            jax.ShapeDtypeStruct((steps, nx, ny, nz), f32),
            jax.ShapeDtypeStruct((steps, nx, ny, nz), f32),
            jax.ShapeDtypeStruct((table_rows, ROWS), f32),
        ),
        in_specs=[smem, any_space, any_space],
        out_specs=(any_space, any_space, vmem),
        scratch_shapes=[
            pltpu.VMEM((order,) + grown, f32),
            pltpu.VMEM((steps,) + grown, f32),
            pltpu.VMEM(coefs.shape, f32),
            pltpu.VMEM((table_rows, ROWS), f32),
            pltpu.VMEM((n_gx, table_rows, ROWS), f32),
            pltpu.VMEM((n_gy, table_rows, ROWS), f32),
            dma((3,)),
            dma((2, steps)),
            dma((4 * steps,)),
            dma((4 * steps,)),
            dma((4 * steps,)),
            dma((4 * steps,)),
            dma((n_gx,)),
            dma((n_gx,)),
            dma((n_gy,)),
            dma((n_gy,)),
        ],
        compiler_params=pltpu.CompilerParams(
            collective_id=0, has_side_effects=True, vmem_limit_bytes=40 * 2**20
        ),
        name="basis",
    )(shifts, rhs, coefs)

    cells = float(nx * ny * nz * n_gx * n_gy)
    planes = 2 if nx % 2 == 0 else 1
    field = pl.BlockSpec((planes, ny, nz), lambda p: (p, 0, 0))
    stack = lambda count: pl.BlockSpec((count, planes, ny, nz), lambda p: (0, p, 0, 0))
    basis, factor, solved, residual = pl.pallas_call(
        functools.partial(combine_kernel, cells),
        grid=(nx // planes,),
        out_shape=(
            jax.ShapeDtypeStruct((order, nx, ny, nz), f32),
            jax.ShapeDtypeStruct((order, order), f32),
            jax.ShapeDtypeStruct((nx, ny, nz), f32),
            jax.ShapeDtypeStruct((nx, ny, nz), f32),
        ),
        in_specs=[smem, pl.BlockSpec((table_rows, ROWS), lambda p: (0, 0)), field, stack(steps), stack(steps)],
        out_specs=(stack(order), pl.BlockSpec((order, order), lambda p: (0, 0)), field, field),
        scratch_shapes=[pltpu.VMEM((order * (order + 1) // 2 + steps + order, 8, ROWS), f32)],
        compiler_params=pltpu.CompilerParams(
            dimension_semantics=("arbitrary",), vmem_limit_bytes=40 * 2**20
        ),
        name="combine",
    )(shifts, gram, rhs, v, w)
    return basis, factor, solved, residual


def solution(mesh):
    placed = (P("gx", "gy", None), P(None, "gx", "gy", None), P())
    return jax.shard_map(
        functools.partial(device_body, mesh.shape["gx"], mesh.shape["gy"]),
        mesh=mesh,
        in_specs=placed,
        out_specs=(P(None, "gx", "gy", None), P(), P("gx", "gy", None), P("gx", "gy", None)),
        check_vma=False,
    )
```

profile of v0, /device:TPU:0, one launch (start us, length us, event | category | flops | bytes accessed | tf_op | source)
XLA Modules:
  0.0 61.7 jit_solution(12256026355844365076)
XLA Ops:
  0.6 0.0 copy-start
  0.6 2.9 %copy-done = f32[13,8,64,256]{3,2,1,0:T(8,128)S(1)} copy-done((f32[13,8,64,256]{3,2,1,0:T(8,128)S(1)}, f32[13,8,64,256]{3,2,1,0:T(8,128)}, u32[]{:S(2)}) %copy-start) | copy-done | bytes 6815768
  3.6 0.0 copy-start.1
  3.6 1.0 %copy-done.1 = f32[8,64,256]{2,1,0:T(8,128)S(1)} copy-done((f32[8,64,256]{2,1,0:T(8,128)S(1)}, f32[8,64,256]{2,1,0:T(8,128)}, u32[]{:S(2)}) %copy-start.1) | copy-done | bytes 524312
  4.6 0.0 copy-start.2
  4.6 0.7 %copy-done.2 = f32[4]{0:T(128)S(1)} copy-done((f32[4]{0:T(128)S(1)}, f32[4]{0:T(128)}, u32[]{:S(2)}) %copy-start.2) | copy-done | bytes 40
  5.3 52.7 %basis.1 = (f32[4,8,64,256]{3,2,1,0:T(8,128)S(1)}, f32[4,8,64,256]{3,2,1,0:T(8,128)S(1)}, f32[32,128]{1,0:T(8,128)S(1)}) custom-call(f32[4]{0:T(128)S(1)} %copy-done.2, f32[8,64,256]{2,1,0:T(8,128)S(1)} %copy-done.1, f32[13,8,64,256]{3,2,1,0:T(8,128)S(1)} %copy-done), custom_call_target="tpu_custom_call" | custom-call | tf_op jit(solution)/shard_map/basis/pallas_call | solution.py:391
  58.0 3.7 %combine.1 = (f32[5,8,64,256]{3,2,1,0:T(8,128)}, f32[5,5]{1,0:T(8,128)}, f32[8,64,256]{2,1,0:T(8,128)}, f32[8,64,256]{2,1,0:T(8,128)}) custom-call(f32[4]{0:T(128)S(1)} %copy-done.2, f32[32,128]{1,0:T(8,128)S(1)} %get-tuple-element.7.gram, f32[8,64,256]{2,1,0:T(8,128)S(1)} %copy-done.1, f32[4,8,64,256]{3,2,1,0:T(8,128)S(1)} %get-tuple-element.8.v, ...), custom_call_target="tpu_custom_call" | custom-call | tf_op jit(solution)/shard_map/combine/pallas_call | solution.py:428
Async XLA Ops:
  0.6 2.9 %copy-start = (f32[13,8,64,256]{3,2,1,0:T(8,128)S(1)}, f32[13,8,64,256]{3,2,1,0:T(8,128)}, u32[]{:S(2)}) copy-start(f32[13,8,64,256]{3,2,1,0:T(8,128)} %coefs.1) | copy-start | bytes 20447236
  3.6 1.0 %copy-start.1 = (f32[8,64,256]{2,1,0:T(8,128)S(1)}, f32[8,64,256]{2,1,0:T(8,128)}, u32[]{:S(2)}) copy-start(f32[8,64,256]{2,1,0:T(8,128)} %rhs.3) | copy-start | bytes 1572868
  4.6 0.7 %copy-start.2 = (f32[4]{0:T(128)S(1)}, f32[4]{0:T(128)}, u32[]{:S(2)}) copy-start(f32[4]{0:T(128)} %shifts.3) | copy-start | bytes 52
where the time goes:
time: 61.9 us; the launch traced here: 61.7 us
  Pallas kernels  56.4 us (91%)
  local copies, waits for them, and re-layouts  4.62 us (7%)
  between operations  0.65 us (1%)
    pallas_call x1, Pallas kernels, device_body(): pl.pallas_call(functools.partial(basis_kernel, n_gx, n_gy), out_shape=(ja...  52.7 us
    unnamed x6, local copies, waits for them, and re-layouts  4.62 us
    pallas_call x1, Pallas kernels, device_body(): pl.pallas_call(functools.partial(combine_kernel, cells), grid=(nx // plan...  3.7 us

commit v1 on v0

v1 whole, which is shorter than its diff:
```python
import functools

import jax
import jax.numpy as jnp
from jax import lax
from jax.experimental import pallas as pl
from jax.experimental.pallas import tpu as pltpu
from jax.sharding import PartitionSpec as P

growth = 2.0
MESH = pl.DeviceIdType.MESH
PAD = 8
ROWS = 128


def basis_kernel(
    n_gx, n_gy, shifts_hbm, rhs, coefs, v_out, w_out, gram,
    field_v, field_w, weight, part, gx_part, gy_part, shifts, y_out, y_in,
    load_sem, store_sem, xs, xr, ys, yr, gxs, gxr, gys, gyr,
):
    steps = shifts.shape[0]
    nx, ny, nz = rhs.shape
    mine = slice(1, nx + 1)
    body = slice(PAD, PAD + ny)
    gx, gy = lax.axis_index("gx"), lax.axis_index("gy")
    x_up, x_down = lax.rem(gx + 1, n_gx), lax.rem(gx + n_gx - 1, n_gx)
    has_low, has_high = gy > 0, gy < n_gy - 1

    loads = [
        pltpu.make_async_copy(rhs, field_v.at[0, mine, body, :], load_sem.at[0]),
        pltpu.make_async_copy(coefs.at[0:7], weight.at[0:7], load_sem.at[1]),
        pltpu.make_async_copy(coefs.at[7:13], weight.at[7:13], load_sem.at[2]),
        pltpu.make_async_copy(shifts_hbm, shifts, load_sem.at[3]),
    ]
    for load in loads:
        load.start()

    barrier = pltpu.get_barrier_semaphore()

    def greet_gx(d, c):
        pl.semaphore_signal(barrier, inc=1, device_id={"gx": lax.rem(gx + d, n_gx)}, device_id_type=MESH)
        return c

    def greet_gy(d, c):
        pl.semaphore_signal(barrier, inc=1, device_id={"gy": lax.rem(gy + d, n_gy)}, device_id_type=MESH)
        return c

    lax.fori_loop(1, n_gx, greet_gx, 0)
    lax.fori_loop(1, n_gy, greet_gy, 0)

    part[...] = jnp.zeros_like(part)

    def clear(fields, rows):
        for k in range(steps):
            for p in range(1, nx + 1):
                fields[k, p, rows, :] = jnp.zeros((PAD, nz), jnp.float32)

    @pl.when(jnp.logical_not(has_low))
    def _():
        clear(field_v, slice(0, PAD))
        clear(field_w, slice(0, PAD))

    @pl.when(jnp.logical_not(has_high))
    def _():
        clear(field_v, slice(PAD + ny, PAD + ny + PAD))
        clear(field_w, slice(PAD + ny, PAD + ny + PAD))

    pl.semaphore_wait(barrier, n_gx + n_gy - 2)

    chunk = ny // 4 if ny % 32 == 0 else ny
    pieces = ny // chunk
    order = [c for c in range(pieces) if 0 < c < pieces - 1] + sorted({0, pieces - 1})

    def x_copy(fields, k, which, side, c, source=None):
        slot = pieces * (2 * steps * which + 2 * k + side) + c
        rows = slice(PAD + c * chunk, PAD + (c + 1) * chunk)
        if source is None:
            source = fields.at[k, 1 if side == 0 else nx, rows, :]
        return pltpu.make_async_remote_copy(
            src_ref=source,
            dst_ref=fields.at[k, nx + 1 if side == 0 else 0, rows, :],
            send_sem=xs.at[slot],
            recv_sem=xr.at[slot],
            device_id={"gx": x_down if side == 0 else x_up},
            device_id_type=MESH,
        )

    def y_copy(k, which, side):
        slot = 2 * steps * which + 2 * k + side
        return pltpu.make_async_remote_copy(
            src_ref=y_out.at[slot],
            dst_ref=y_in.at[slot],
            send_sem=ys.at[slot],
            recv_sem=yr.at[slot],
            device_id={"gy": jnp.maximum(gy - 1, 0) if side == 0 else jnp.minimum(gy + 1, n_gy - 1)},
            device_id_type=MESH,
        )

    def y_start(fields, k, which):
        for side, there in ((0, has_low), (1, has_high)):
            slot = 2 * steps * which + 2 * k + side
            row = PAD if side == 0 else PAD + ny - 1

            @pl.when(there)
            def _():
                for p in range(nx):
                    y_out[slot, p : p + 1, :] = fields[k, p + 1, row : row + 1, :]
                y_copy(k, which, side).start()

    def y_arrived(fields, k, which):
        for side, there in ((1, has_low), (0, has_high)):
            slot = 2 * steps * which + 2 * k + side
            row = PAD + ny if side == 0 else PAD - 1

            @pl.when(there)
            def _():
                y_copy(k, which, side).wait_recv()
                for p in range(nx):
                    fields[k, p + 1, row : row + 1, :] = y_in[slot, p : p + 1, :]

    def near(fields, k, p, r, rows):
        centre = fields[k, p + 1, PAD + r : PAD + r + rows, :]
        lane = lax.broadcasted_iota(jnp.int32, centre.shape, 1)
        return centre, (
            fields[k, p, PAD + r : PAD + r + rows, :],
            fields[k, p + 2, PAD + r : PAD + r + rows, :],
            fields[k, p + 1, PAD + r - 1 : PAD + r - 1 + rows, :],
            fields[k, p + 1, PAD + r + 1 : PAD + r + 1 + rows, :],
            jnp.where(lane == 0, 0.0, pltpu.roll(centre, 1, 1)),
            jnp.where(lane == nz - 1, 0.0, pltpu.roll(centre, nz - 1, 1)),
        )

    def block_m(k, p, r, rows):
        centre, sides = near(field_v, k, p, r, rows)
        total = weight[0, p, r : r + rows, :] * centre
        for d in range(6):
            total = total + weight[1 + d, p, r : r + rows, :] * sides[d]
        field_w[k, p + 1, PAD + r : PAD + r + rows, :] = total

    def block_a(k, p, r, rows):
        centre, sides = near(field_w, k, p, r, rows)
        total = centre
        for d in range(6):
            total = total - weight[7 + d, p, r : r + rows, :] * sides[d]
        old = field_v[k, p + 1, PAD + r : PAD + r + rows, :]
        field_v[k + 1, p + 1, PAD + r : PAD + r + rows, :] = growth * (total - shifts[k] * old)

    def apply(block, fields, k, which, out, out_k, out_which, send):
        for c in order:
            if c == 0:
                y_arrived(fields, k, which)
            for side in range(2):
                x_copy(fields, k, which, 1 - side, c).wait_recv()
                block(k, 0 if side == 0 else nx - 1, c * chunk, chunk)

                @pl.when(send)
                def _():
                    x_copy(out, out_k, out_which, side, c).start()

        def edge(p, c):
            block(k, p, 0, 8)
            block(k, p, ny - 8, 8)
            return c

        lax.fori_loop(1, nx - 1, edge, 0)

        @pl.when(send)
        def _():
            y_start(out, out_k, out_which)

        def inner(p, c):
            for r in range(8, ny - 8, 16):
                block(k, p, r, min(16, ny - 8 - r))
            return c

        lax.fori_loop(1, nx - 1, inner, 0)

    def products(i):
        def one(j, c):
            def add(p, total):
                a = field_v[i, p + 1, body, :]
                b = field_v[j, p + 1, body, :]
                return total + jnp.sum((a * b).reshape(ny // 8, 8, nz), axis=0)

            total = lax.fori_loop(0, nx, add, jnp.zeros((8, nz), jnp.float32))
            row = jnp.sum(total, axis=0, keepdims=True)
            flat = row[:, :ROWS]
            for q in range(1, nz // ROWS):
                flat = flat + row[:, q * ROWS : (q + 1) * ROWS]
            part[pl.ds(i * (i + 1) // 2 + j, 1), :] = flat
            return c

        lax.fori_loop(0, i + 1, one, 0)

    for c in order:
        for side in range(2):
            plane = rhs.at[0 if side == 0 else nx - 1, c * chunk : (c + 1) * chunk, :]
            x_copy(field_v, 0, 0, side, c, plane).start()
    loads[0].wait()
    y_start(field_v, 0, 0)
    products(0)
    for load in loads[1:]:
        load.wait()

    def v_store(k):
        return pltpu.make_async_copy(field_v.at[k, mine, body, :], v_out.at[k], store_sem.at[0, k])

    def w_store(k):
        return pltpu.make_async_copy(field_w.at[k, mine, body, :], w_out.at[k], store_sem.at[1, k])

    def step(k, c):
        apply(block_m, field_v, k, 0, field_w, k, 1, k >= 0)
        w_store(k).start()
        apply(block_a, field_w, k, 1, field_v, k + 1, 0, k + 1 < steps)
        v_store(k + 1).start()
        products(k + 1)
        return c

    v_store(0).start()
    lax.fori_loop(0, steps, step, 0)

    def gather(axis, me, n, store, send_sem, recv_sem, value):
        store[me] = value

        def copy(d):
            return pltpu.make_async_remote_copy(
                src_ref=store.at[me],
                dst_ref=store.at[me],
                send_sem=send_sem.at[d],
                recv_sem=recv_sem.at[d],
                device_id={axis: lax.rem(me + d, n)},
                device_id_type=MESH,
            )

        def start(d, c):
            copy(d).start()
            return c

        def arrive(d, c):
            copy(d).wait_recv()
            return c

        def sent(d, c):
            copy(d).wait_send()
            return c

        lax.fori_loop(1, n, start, 0)
        lax.fori_loop(1, n, arrive, 0)
        total = lax.fori_loop(0, n, lambda s, t: t + store[s], jnp.zeros_like(value))
        return total, lambda: lax.fori_loop(1, n, sent, 0)

    half = part.shape[0] // 2
    sums = jnp.sum(part[...], axis=1, keepdims=True)
    left = lax.broadcasted_iota(jnp.int32, (half, ROWS), 1) < ROWS // 2
    packed = jnp.where(left, jnp.broadcast_to(sums[:half], left.shape), jnp.broadcast_to(sums[half:], left.shape))
    total, done_x = gather("gx", gx, n_gx, gx_part, gxs, gxr, packed)
    total, done_y = gather("gy", gy, n_gy, gy_part, gys, gyr, total)
    gram[0:half, :] = total
    for k in range(steps):
        gram[half + k : half + k + 1, :] = jnp.full((1, ROWS), shifts[k], jnp.float32)
    done_x()
    done_y()

    def finish(k, c):
        for which, fields in ((0, field_v), (1, field_w)):
            for side in range(2):
                for piece in range(pieces):
                    x_copy(fields, k, which, side, piece).wait_send()

            @pl.when(has_low)
            def _():
                y_copy(k, which, 0).wait_send()

            @pl.when(has_high)
            def _():
                y_copy(k, which, 1).wait_send()

        v_store(k).wait()
        w_store(k).wait()
        return c

    lax.fori_loop(0, steps, finish, 0)
    v_store(steps).wait()


def small_algebra(gram, steps, cells):
    order = steps + 1
    half = gram.shape[0] // 2
    shifts = [gram[half + k : half + k + 1, :] for k in range(steps)]
    sums = gram[:half] / cells
    turned = pltpu.roll(sums, ROWS // 2, 1)
    left = lax.broadcasted_iota(jnp.int32, sums.shape, 1) < ROWS // 2
    sums = (jnp.where(left, sums, turned), jnp.where(left, turned, sums))

    def entry(i, j):
        n = max(i, j) * (max(i, j) + 1) // 2 + min(i, j)
        return sums[n // half][n % half : n % half + 1, :]

    factor = {}
    for i in range(order):
        value = entry(i, i)
        for k in range(i):
            value = value - factor[k, i] * factor[k, i]
        factor[i, i] = jnp.sqrt(value)
        for j in range(i + 1, order):
            value = entry(i, j)
            for k in range(i):
                value = value - factor[k, i] * factor[k, j]
            factor[i, j] = value / factor[i, i]
    inverse = {}
    for j in range(order):
        inverse[j, j] = 1.0 / factor[j, j]
        for i in range(j - 1, -1, -1):
            value = factor[i, i + 1] * inverse[i + 1, j]
            for k in range(i + 2, j + 1):
                value = value + factor[i, k] * inverse[k, j]
            inverse[i, j] = -value / factor[i, i]
    zero = jnp.zeros_like(factor[0, 0])

    def upper(i, j):
        return factor.get((i, j), zero)

    hess = [[upper(i, k) * shifts[k] + upper(i, k + 1) * (1.0 / growth) for k in range(steps)] for i in range(order)]
    target = [upper(i, 0) for i in range(order)]
    for k in range(steps):
        top, below = hess[k][k], hess[k + 1][k]
        radius = jnp.sqrt(top * top + below * below)
        cosine, sine = top / radius, below / radius
        for c in range(k, steps):
            a, b = hess[k][c], hess[k + 1][c]
            hess[k][c] = cosine * a + sine * b
            hess[k + 1][c] = cosine * b - sine * a
        a, b = target[k], target[k + 1]
        target[k] = cosine * a + sine * b
        target[k + 1] = cosine * b - sine * a
    weights = [None] * steps
    for i in range(steps - 1, -1, -1):
        value = target[i]
        for k in range(i + 1, steps):
            value = value - hess[i][k] * weights[k]
        weights[i] = value / hess[i][i]
    combine = []
    for j in range(order):
        value = zero + (1.0 if j == 0 else 0.0)
        if j < steps:
            value = value - shifts[j] * weights[j]
        if j > 0:
            value = value - (1.0 / growth) * weights[j - 1]
        combine.append(value)
    return factor, inverse, weights, combine


def combine_kernel(cells, gram, v, w, basis, factor_out, solution_out, residual, table, basis_v, sol_v, res_v, sem):
    order, nx, ny, nz = v.shape
    steps = order - 1
    pairs = [(j, k) for k in range(order) for j in range(k + 1)]
    tail = len(pairs)

    factor, inverse, weights, combine = small_algebra(gram[...], steps, cells)
    values = [inverse[p] for p in pairs] + weights + combine
    for n, value in enumerate(values):
        table[n] = jnp.broadcast_to(value, table.shape[1:])
    row = lax.broadcasted_iota(jnp.int32, (8, ROWS), 0)
    column = lax.broadcasted_iota(jnp.int32, (8, ROWS), 1)
    whole = jnp.zeros((8, ROWS), jnp.float32)
    for (i, j), value in factor.items():
        whole = jnp.where((row == i) & (column == j), value, whole)
    factor_out[...] = whole[:order, :order]

    def mul(n, x):
        return table[n][None] * x

    deep = 16 if ny % 16 == 0 else 8

    def tile(p, t):
        rows = pl.ds(pl.multiple_of(t * deep, deep), deep)
        for q in range(0, nz, ROWS):
            lanes = slice(q, q + ROWS)
            load = lambda x: x.reshape(deep // 8, 8, ROWS)
            fields = [load(v[k, p, rows, lanes]) for k in range(order)]
            for k in range(order):
                total = None
                for j in range(k + 1):
                    term = mul(pairs.index((j, k)), fields[j])
                    total = term if total is None else total + term
                basis_v[k, p, rows, lanes] = total.reshape(deep, ROWS)
            total = mul(tail, load(w[0, p, rows, lanes]))
            for k in range(1, steps):
                total = total + mul(tail + k, load(w[k, p, rows, lanes]))
            sol_v[p, rows, lanes] = total.reshape(deep, ROWS)
            total = mul(tail + steps, fields[0])
            for j in range(1, order):
                total = total + mul(tail + steps + j, fields[j])
            res_v[p, rows, lanes] = total.reshape(deep, ROWS)

    def copies(p):
        return (
            pltpu.make_async_copy(basis_v.at[:, p], basis.at[:, p], sem.at[p, 0]),
            pltpu.make_async_copy(sol_v.at[p], solution_out.at[p], sem.at[p, 1]),
            pltpu.make_async_copy(res_v.at[p], residual.at[p], sem.at[p, 2]),
        )

    def plane(p, c):
        def inner(t, d):
            tile(p, t)
            return d

        lax.fori_loop(0, ny // deep, inner, 0)
        for copy in copies(p):
            copy.start()
        return c

    def finish(p, c):
        for copy in copies(p):
            copy.wait()
        return c

    lax.fori_loop(0, nx, plane, 0)
    lax.fori_loop(0, nx, finish, 0)


def device_body(n_gx, n_gy, rhs, coefs, shifts):
    steps = shifts.shape[0]
    order = steps + 1
    nx, ny, nz = rhs.shape
    f32 = jnp.float32
    grown = (nx + 2, ny + 2 * PAD, nz)
    half = -(-(order * (order + 1) // 2) // 16) * 8
    pieces = 4 if ny % 32 == 0 else 1
    hbm = pl.BlockSpec(memory_space=pltpu.HBM)
    any_space = pl.BlockSpec(memory_space=pl.ANY)
    vmem = pl.BlockSpec(memory_space=pltpu.VMEM)
    dma = pltpu.SemaphoreType.DMA
    halo = 4 * steps
    rhs = pltpu.with_memory_space_constraint(rhs, pltpu.HBM)
    coefs = pltpu.with_memory_space_constraint(coefs, pltpu.HBM)
    shifts = pltpu.with_memory_space_constraint(shifts, pltpu.HBM)
    v, w, gram = pl.pallas_call(
        functools.partial(basis_kernel, n_gx, n_gy),
        out_shape=(
            jax.ShapeDtypeStruct((order, nx, ny, nz), f32),
            jax.ShapeDtypeStruct((steps, nx, ny, nz), f32),
            jax.ShapeDtypeStruct((2 * half, ROWS), f32),
        ),
        in_specs=[hbm, hbm, hbm],
        out_specs=(any_space, any_space, vmem),
        scratch_shapes=[
            pltpu.VMEM((order,) + grown, f32),
            pltpu.VMEM((steps,) + grown, f32),
            pltpu.VMEM(coefs.shape, f32),
            pltpu.VMEM((2 * half, ROWS), f32),
            pltpu.VMEM((n_gx, half, ROWS), f32),
            pltpu.VMEM((n_gy, half, ROWS), f32),
            pltpu.SMEM(shifts.shape, f32),
            pltpu.VMEM((halo, nx, nz), f32),
            pltpu.VMEM((halo, nx, nz), f32),
            dma((4,)),
            dma((2, order)),
            dma((halo * pieces,)),
            dma((halo * pieces,)),
            dma((halo,)),
            dma((halo,)),
            dma((n_gx,)),
            dma((n_gx,)),
            dma((n_gy,)),
            dma((n_gy,)),
        ],
        compiler_params=pltpu.CompilerParams(
            collective_id=0, has_side_effects=True, vmem_limit_bytes=32 * 2**20
        ),
        name="basis",
    )(shifts, rhs, coefs)

    cells = float(nx * ny * nz * n_gx * n_gy)
    return pl.pallas_call(
        functools.partial(combine_kernel, cells),
        out_shape=(
            jax.ShapeDtypeStruct((order, nx, ny, nz), f32),
            jax.ShapeDtypeStruct((order, order), f32),
            jax.ShapeDtypeStruct((nx, ny, nz), f32),
            jax.ShapeDtypeStruct((nx, ny, nz), f32),
        ),
        in_specs=[vmem, vmem, vmem],
        out_specs=(hbm, vmem, hbm, hbm),
        scratch_shapes=[
            pltpu.VMEM((order * (order + 1) // 2 + steps + order, 8, ROWS), f32),
            pltpu.VMEM((order, nx, ny, nz), f32),
            pltpu.VMEM((nx, ny, nz), f32),
            pltpu.VMEM((nx, ny, nz), f32),
            dma((nx, 3)),
        ],
        compiler_params=pltpu.CompilerParams(vmem_limit_bytes=32 * 2**20),
        name="combine",
    )(gram, v, w)


def solution(mesh):
    placed = (P("gx", "gy", None), P(None, "gx", "gy", None), P())
    return jax.shard_map(
        functools.partial(device_body, mesh.shape["gx"], mesh.shape["gy"]),
        mesh=mesh,
        in_specs=placed,
        out_specs=(P(None, "gx", "gy", None), P(), P("gx", "gy", None), P("gx", "gy", None)),
        check_vma=False,
    )
```

time: 61.9 us -> 54.6 us (0.88)
  local copies, waits for them, and re-layouts: 4.62 us -> 0 us
  Pallas kernels: 56.4 us -> 53.8 us
    unnamed x6 -> x0, local copies, waits for them, and re-layouts: 4.62 us -> none
    pallas_call x1, Pallas kernels: 52.7 us -> 50.8 us  [device_body(): pl.pallas_call(functools.partial(basis_kernel, n_gx, n_gy), out_shape=(ja...]
    pallas_call x1, Pallas kernels: 3.7 us -> 2.94 us  [device_body(): pl.pallas_call(functools.partial(combine_kernel, cells), out_shape=(jax.S...]
where the time goes in v1:
time: 54.6 us; the launch traced here: 54.4 us
  Pallas kernels  53.8 us (99%)
  between operations  0.64 us (1%)
    pallas_call x1, Pallas kernels, device_body(): pl.pallas_call(functools.partial(basis_kernel, n_gx, n_gy), out_shape=(ja...  50.8 us
    pallas_call x1, Pallas kernels, device_body(): pl.pallas_call(functools.partial(combine_kernel, cells), out_shape=(jax.S...  2.94 us

profile of v1, /device:TPU:0, one launch (start us, length us, event | category | flops | bytes accessed | tf_op | source)
XLA Modules:
  0.0 54.4 jit_solution(8356072069650409765)
XLA Ops:
  0.6 50.8 %basis.1 = (f32[5,8,64,256]{3,2,1,0:T(8,128)S(1)}, f32[4,8,64,256]{3,2,1,0:T(8,128)S(1)}, f32[16,128]{1,0:T(8,128)S(1)}) custom-call(f32[4]{0:T(128)} %shifts_hbm.1, f32[8,64,256]{2,1,0:T(8,128)} %rhs.1, f32[13,8,64,256]{3,2,1,0:T(8,128)} %coefs.1), custom_call_target="tpu_custom_call" | custom-call | tf_op jit(solution)/shard_map/basis/pallas_call | solution.py:438
  51.5 2.9 %combine.1 = (f32[5,8,64,256]{3,2,1,0:T(8,128)}, f32[5,5]{1,0:T(8,128)}, f32[8,64,256]{2,1,0:T(8,128)}, f32[8,64,256]{2,1,0:T(8,128)}) custom-call(f32[16,128]{1,0:T(8,128)S(1)} %get-tuple-element.7.gram, f32[5,8,64,256]{3,2,1,0:T(8,128)S(1)} %get-tuple-element.8.v, f32[4,8,64,256]{3,2,1,0:T(8,128)S(1)} %get-tuple-element.9.w), custom_call_target="tpu_custom_call" | custom-call | tf_op jit(solution)/shard_map/combine/pallas_call | solution.py:475

commit v2 on v1

--- a/solution.py
+++ b/solution.py
@@ -146,16 +146,7 @@
         field_v[k + 1, p + 1, PAD + r : PAD + r + rows, :] = growth * (total - shifts[k] * old)
 
     def apply(block, fields, k, which, out, out_k, out_which, send):
-        for c in order:
-            if c == 0:
-                y_arrived(fields, k, which)
-            for side in range(2):
-                x_copy(fields, k, which, 1 - side, c).wait_recv()
-                block(k, 0 if side == 0 else nx - 1, c * chunk, chunk)
-
-                @pl.when(send)
-                def _():
-                    x_copy(out, out_k, out_which, side, c).start()
+        y_arrived(fields, k, which)
 
         def edge(p, c):
             block(k, p, 0, 8)
@@ -163,6 +154,15 @@
             return c
 
         lax.fori_loop(1, nx - 1, edge, 0)
+
+        for c in order:
+            for side in range(2):
+                x_copy(fields, k, which, 1 - side, c).wait_recv()
+                block(k, 0 if side == 0 else nx - 1, c * chunk, chunk)
+
+                @pl.when(send)
+                def _():
+                    x_copy(out, out_k, out_which, side, c).start()
 
         @pl.when(send)
         def _():

time: 54.6 us -> 53.5 us (0.980)
  Pallas kernels: 53.8 us -> 52.7 us
    pallas_call x1, Pallas kernels: 50.8 us -> 49.8 us  [device_body(): pl.pallas_call(functools.partial(basis_kernel, n_gx, n_gy), out_shape=(ja...]
where the time goes in v2:
time: 53.5 us; the launch traced here: 53.4 us
  Pallas kernels  52.7 us (99%)
  between operations  0.64 us (1%)
    pallas_call x1, Pallas kernels, device_body(): pl.pallas_call(functools.partial(basis_kernel, n_gx, n_gy), out_shape=(ja...  49.8 us
    pallas_call x1, Pallas kernels, device_body(): pl.pallas_call(functools.partial(combine_kernel, cells), out_shape=(jax.S...  2.94 us

profile of v2, /device:TPU:0, one launch (start us, length us, event | category | flops | bytes accessed | tf_op | source)
XLA Modules:
  0.0 53.4 jit_solution(2022885610026661142)
XLA Ops:
  0.6 49.8 %basis.1 = (f32[5,8,64,256]{3,2,1,0:T(8,128)S(1)}, f32[4,8,64,256]{3,2,1,0:T(8,128)S(1)}, f32[16,128]{1,0:T(8,128)S(1)}) custom-call(f32[4]{0:T(128)} %shifts_hbm.1, f32[8,64,256]{2,1,0:T(8,128)} %rhs.1, f32[13,8,64,256]{3,2,1,0:T(8,128)} %coefs.1), custom_call_target="tpu_custom_call" | custom-call | tf_op jit(solution)/shard_map/basis/pallas_call | solution.py:438
  50.4 2.9 %combine.1 = (f32[5,8,64,256]{3,2,1,0:T(8,128)}, f32[5,5]{1,0:T(8,128)}, f32[8,64,256]{2,1,0:T(8,128)}, f32[8,64,256]{2,1,0:T(8,128)}) custom-call(f32[16,128]{1,0:T(8,128)S(1)} %get-tuple-element.7.gram, f32[5,8,64,256]{3,2,1,0:T(8,128)S(1)} %get-tuple-element.8.v, f32[4,8,64,256]{3,2,1,0:T(8,128)S(1)} %get-tuple-element.9.w), custom_call_target="tpu_custom_call" | custom-call | tf_op jit(solution)/shard_map/combine/pallas_call | solution.py:475
